TPU v7x, 512 devices: a whole 4x4x16 slice. The times are simulated.
512 devices in a mesh: row: 32 (over z_hi, y, core), col: 16 (over z_lo, x).
Axes of the slice: x: 4, y: 4, z: 16 (z_hi: 4, z_lo: 4; z = z_hi * 4 + z_lo), core: 2. Of those that a mesh axis runs over, the one named last changes fastest.
Arguments:
- hidden: bfloat16 [256, 2048], P('row', 'col'), may hold values from -60 to 60
- queries: bfloat16 [256, 4096], P('row'), may hold values from -6 to 6
- new_kv: bfloat16 [256, 2, 2048], P('row'), may hold values from -12 to 12
- prompt_kv: bfloat16 [32, 2, 1024, 2048], P('row', None, 'col'), may hold values from -180 to 180
- suffix_kv: bfloat16 [256, 2, 128, 2048], P('row', None, 'col'), may hold values from -12 to 12
- lengths: int32 [256], P('row'), may hold values from 1 to 128, as said below
- w_out: bfloat16 [4096, 2048], P(None, 'col'), may hold values from -0.375 to 0.375
- moe_gain: bfloat16 [2048], P('col'), may hold values from 0.099609375 to 1.8984375
- w_router: bfloat16 [2048, 8], P('col'), may hold values from -0.5 to 0.5
- expert_weights: bfloat16 [8, 5632, 3, 2048], P(None, 'row', None, 'col'), may hold values from -0.25 to 0.25
- old_lines: int32 [8, 5632], replicated, may hold values from 0 to 5631, as said below
- new_lines: int32 [8, 5632], replicated, may hold values from 0 to 5631, as said below
- routes: int32 [256, 2], replicated, may hold values from 0 to 7, all different within a row
Outputs:
- layer_out: float32 [256, 2048], P('row', 'col')
- moved_weights: bfloat16 [8, 5632, 3, 2048], P(None, 'row', None, 'col')
Inputs may be any that keep to these rules, and one draw needn't show every extreme that they name: `lengths`: some sequence has all 128 slots filled. `old_lines`: each row is a permutation of the hidden units of one expert; stored lines [j * 176, (j + 1) * 176) lie on row index j. `new_lines`: each row is a permutation of the hidden units of one expert. Counting all experts together, exactly 44 of the lines that one row index holds under old_lines are held by each row index under new_lines. `routes`: the two experts of a token differ.
All inputs are finite; a program needn't handle non-finite values.
Results may differ from a plain program's by a relative error of at most 0.04.
Values may be sent and summed in bfloat16 or wider, within the bound.
A program may use at most 64 MiB of HBM per device.

v0:
```python
import jax
import jax.numpy as jnp
from jax import lax
from jax.sharding import PartitionSpec as P

D = 2048
KVH = 16
HD = 128
REP = 2
norm_eps = 1e-06
neg_big = -1e30


def joined(part, axis, combine):
    gathered = jax.tree.map(lambda a: lax.all_gather(a, axis), part)

    def take(source):
        return jax.tree.map(lambda a: lax.dynamic_index_in_dim(a, source, 0, False), gathered)

    return lax.fori_loop(
        1, lax.axis_size(axis), lambda source, state: combine(state, take(source)), take(0)
    )


def merge_partial(earlier, following):
    highest_a, totals_a, mixture_a = earlier
    highest_b, totals_b, mixture_b = following
    highest = jnp.maximum(highest_a, highest_b)
    factor_a = jnp.exp(highest_a - highest)
    factor_b = jnp.exp(highest_b - highest)
    return (
        highest,
        totals_a * factor_a + totals_b * factor_b,
        mixture_a * factor_a[..., None] + mixture_b * factor_b[..., None],
    )


def attend(queries, new_kv, prompt_kv, suffix_kv, lengths):
    seq_count = queries.shape[0]
    prompt_rows = prompt_kv.shape[2]
    suffix_rows = suffix_kv.shape[2]
    col_index = lax.axis_index("col")
    query_heads = queries.reshape(seq_count, KVH, REP, HD)
    prompt_keys = prompt_kv[0, 0].reshape(prompt_rows, KVH, HD)
    prompt_values = prompt_kv[0, 1].reshape(prompt_rows, KVH, HD)
    suffix_keys = suffix_kv[:, 0].reshape(seq_count, suffix_rows, KVH, HD)
    suffix_values = suffix_kv[:, 1].reshape(seq_count, suffix_rows, KVH, HD)
    own_keys = new_kv[:, 0].reshape(seq_count, KVH, HD)
    own_values = new_kv[:, 1].reshape(seq_count, KVH, HD)
    score_scale = HD ** (-0.5)
    prompt_scores = (
        jnp.einsum("skgd,pkd->skgp", query_heads, prompt_keys, preferred_element_type=jnp.float32)
        * score_scale
    )
    suffix_scores = (
        jnp.einsum("skgd,spkd->skgp", query_heads, suffix_keys, preferred_element_type=jnp.float32)
        * score_scale
    )
    own_scores = (
        jnp.einsum("skgd,skd->skg", query_heads, own_keys, preferred_element_type=jnp.float32)
        * score_scale
    )
    positions = col_index * suffix_rows + jnp.arange(suffix_rows, dtype=jnp.int32)
    live_slots = (positions[None, :] < lengths[:, None])[:, None, None, :]
    holder = col_index == 0
    suffix_scores = jnp.where(live_slots, suffix_scores, neg_big)
    own_scores = jnp.where(holder, own_scores, neg_big)
    highest = jnp.maximum(
        jnp.maximum(jnp.max(prompt_scores, axis=-1), jnp.max(suffix_scores, axis=-1)), own_scores
    )
    prompt_weights = jnp.exp(prompt_scores - highest[..., None])
    suffix_weights = jnp.where(live_slots, jnp.exp(suffix_scores - highest[..., None]), 0.0)
    own_weights = jnp.where(holder, jnp.exp(own_scores - highest), 0.0)
    totals = jnp.sum(prompt_weights, axis=-1) + jnp.sum(suffix_weights, axis=-1) + own_weights
    mixture = jnp.einsum(
        "skgp,pkd->skgd",
        prompt_weights.astype(jnp.bfloat16),
        prompt_values,
        preferred_element_type=jnp.float32,
    )
    mixture = mixture + jnp.einsum(
        "skgp,spkd->skgd",
        suffix_weights.astype(jnp.bfloat16),
        suffix_values,
        preferred_element_type=jnp.float32,
    )
    own_rounded = lax.optimization_barrier(own_weights.astype(jnp.bfloat16)).astype(jnp.float32)
    mixture = mixture + own_rounded[..., None] * own_values.astype(jnp.float32)[:, :, None, :]
    highest, totals, mixture = joined((highest, totals, mixture), "col", merge_partial)
    return (mixture / totals[..., None]).astype(jnp.bfloat16).reshape(seq_count, -1)


def inverse_rows(table):
    expert_count, full_width = table.shape
    row_ids = jnp.broadcast_to(jnp.arange(expert_count, dtype=jnp.int32)[:, None], table.shape)
    slot_ids = jnp.broadcast_to(jnp.arange(full_width, dtype=jnp.int32)[None, :], table.shape)
    return jnp.zeros_like(table).at[row_ids, table].set(slot_ids)


def migrate(expert_weights, old_lines, new_lines):
    row_count = lax.axis_size("row")
    row_index = lax.axis_index("row")
    expert_count, line_count, three_parts, width_col = expert_weights.shape
    full_width = old_lines.shape[1]
    unit_count = expert_count * line_count
    per_peer = unit_count // row_count
    inverse_old = inverse_rows(old_lines)
    inverse_new = inverse_rows(new_lines)
    held_ids = lax.dynamic_slice_in_dim(old_lines, row_index * line_count, line_count, 1)
    target_slots = jnp.take_along_axis(inverse_new, held_ids, axis=1)
    expert_ids = jnp.arange(expert_count, dtype=jnp.int32)[:, None]
    sort_keys = (
        target_slots // line_count * (expert_count * full_width)
        + expert_ids * full_width
        + target_slots
    )
    sort_order = jnp.argsort(sort_keys.reshape(-1))
    flat_units = expert_weights.reshape(unit_count, three_parts, width_col)
    outgoing = flat_units[sort_order].reshape(row_count, per_peer, three_parts, width_col)
    arrived = lax.all_to_all(outgoing, "row", split_axis=0, concat_axis=0, tiled=True).reshape(
        unit_count, three_parts, width_col
    )
    wanted_ids = lax.dynamic_slice_in_dim(new_lines, row_index * line_count, line_count, 1)
    anchor_rows = (jnp.take_along_axis(inverse_old, wanted_ids, axis=1) // line_count).reshape(-1)
    anchor_hits = (anchor_rows[:, None] == jnp.arange(row_count, dtype=jnp.int32)[None, :]).astype(
        jnp.int32
    )
    rank_within = jnp.sum(jnp.cumsum(anchor_hits, axis=0) * anchor_hits, axis=1) - 1
    arrived_slot = anchor_rows * per_peer + rank_within
    return arrived[arrived_slot].reshape(expert_count, line_count, three_parts, width_col)


def activate(summed, router_sum, square_sum, chosen):
    inverse_rms = lax.rsqrt(square_sum / D + norm_eps)
    logits = router_sum * inverse_rms[:, None]
    expert_hits = chosen[:, :, None] == jnp.arange(logits.shape[1], dtype=jnp.int32)[None, None, :]
    selected = jnp.sum(jnp.where(expert_hits, logits[:, None, :], 0.0), axis=-1)
    gates = jax.nn.softmax(selected, axis=-1)
    gate_part = summed[:, :, 0] * inverse_rms[:, None, None]
    up_part = summed[:, :, 1] * inverse_rms[:, None, None]
    activated = (jax.nn.silu(gate_part) * up_part).astype(jnp.bfloat16)
    return (gates, activated)


def local(
    hidden,
    queries,
    new_kv,
    prompt_kv,
    suffix_kv,
    lengths,
    w_out,
    moe_gain,
    w_router,
    expert_weights,
    old_lines,
    new_lines,
    routes,
):
    moved_weights = migrate(expert_weights, old_lines, new_lines)
    attended = attend(queries, new_kv, prompt_kv, suffix_kv, lengths)
    projected = jnp.dot(attended, w_out, preferred_element_type=jnp.float32)
    h_mid = (hidden.astype(jnp.float32) + projected).astype(jnp.bfloat16)
    h_float = h_mid.astype(jnp.float32)
    scaled = (h_float * moe_gain.astype(jnp.float32)[None, :]).astype(jnp.bfloat16)
    squares = jnp.sum(h_float * h_float, axis=1)
    every_token, every_square = (
        lax.all_gather(scaled, "row", axis=0, tiled=True),
        lax.all_gather(squares.astype(jnp.bfloat16), "row", axis=0, tiled=True).astype(
            squares.dtype
        ),
    )
    token_total = every_token.shape[0]
    router_part = jnp.dot(every_token, w_router, preferred_element_type=jnp.float32)
    gate_up = jnp.einsum(
        "td,efjd->etjf",
        every_token,
        expert_weights[:, :, :2, :],
        preferred_element_type=jnp.float32,
    )
    picked = gate_up[routes, jnp.arange(token_total, dtype=jnp.int32)[:, None]]
    summed, router_sum, square_sum = lax.psum((picked, router_part, every_square), "col")
    gates, activated = activate(summed, router_sum, square_sum, routes)
    down_lines = expert_weights[:, :, 2, :]
    top_count = routes.shape[1]
    every_expert = jnp.einsum(
        "tkf,efd->etkd", activated, down_lines, preferred_element_type=jnp.float32
    )
    chosen_out = every_expert[
        routes,
        jnp.arange(hidden.shape[0] * lax.axis_size("row"), dtype=jnp.int32)[:, None],
        jnp.arange(top_count, dtype=jnp.int32)[None, :],
    ]
    mixed = lax.psum_scatter(
        jnp.sum(chosen_out * gates[:, :, None], axis=1), "row", scatter_dimension=0, tiled=True
    )
    layer_out = h_float + mixed
    return (layer_out, moved_weights)


def solution(mesh):
    return jax.shard_map(
        local,
        mesh=mesh,
        in_specs=(
            P("row", "col"),
            P("row", None),
            P("row", None, None),
            P("row", None, "col", None),
            P("row", None, "col", None),
            P("row"),
            P(None, "col"),
            P("col"),
            P("col", None),
            P(None, "row", None, "col"),
            P(),
            P(),
            P(),
        ),
        out_specs=(P("row", "col"), P(None, "row", None, "col")),
        check_vma=False,
    )
```

profile of v0, /device:TPU:1, one launch (start us, length us, event | category | flops | bytes accessed | tf_op | source)
XLA Modules:
  0.0 1099.8 jit_solution(18043587728457277030)
XLA Ops:
  7.3 1.2 fusion.38
  8.6 1.1 slice_bitcast_fusion.2
  12.7 6.7 copy.177
  21.3 165.0 %scatter_custom_fusion = s32[45056]{0:T(1024)S(1)} fusion(s32[45056]{0:T(1024)} %reshape.244, s32[45056]{0:T(1024)} %reshape.246, s32[]{:T(128)} %constant.115.clone.1), kind=kCustom, calls=%fused_computation.72 | custom fusion | bytes 180736
  187.2 8.6 gather_fusion.4
  196.1 5.0 sort.17
  201.1 5.2 gather_fusion.2
  206.3 2.6 copy.179
  208.9 19.4 %all-to-all-start = ((bf16[32,44,3,128]{3,1,2,0:T(8,128)(2,1)}), bf16[32,44,3,128]{3,1,2,0:T(8,128)(2,1)}, u32[]{:S(2)}, u32[]{:S(2)}) async-start(bf16[32,44,3,128]{3,1,2,0:T(8,128)(2,1)} %copy.179), calls=%async_computation | async-start | bytes 2359296 | tf_op jit(solution)/shard_map/all_to_all | solution.py:120
  228.4 165.3 %scatter_custom_fusion.1 = s32[45056]{0:T(1024)S(1)} fusion(s32[45056]{0:T(1024)S(1)} %reshape.250, s32[45056]{0:T(1024)} %reshape.246, s32[]{:T(128)} %constant.115.clone.1), kind=kCustom, calls=%fused_computation.70 | custom fusion | bytes 180736
  393.9 8.6 gather_fusion.5
  403.6 34.4 %all-gather = f32[128,16,2]{1,2,0:T(2,128)S(1)} all-gather(f32[8,16,2]{1,2,0:T(2,128)S(1)} %copy.156), channel_id=2, replica_groups=mesh['row'=32,'col'=16] {'col'}, dimensions={0}, use_global_device_ids=true | all-gather | bytes 17408 | tf_op jit(solution)/shard_map/all_gather | solution.py:15
  438.9 30.4 %all-gather.1 = f32[128,16,2]{1,2,0:T(2,128)S(1)} all-gather(f32[8,16,2]{1,2,0:T(2,128)S(1)} %copy.161), channel_id=3, replica_groups=mesh['row'=32,'col'=16] {'col'}, dimensions={0}, use_global_device_ids=true | all-gather | bytes 17408 | tf_op jit(solution)/shard_map/all_gather | solution.py:15
  470.6 9.1 reduce-window.6
  481.6 0.9 slice.69
  482.6 30.4 %while.19 = (s32[]{:T(128)}, f32[8,16,2]{1,2,0:T(2,128)S(1)}, f32[8,16,2]{1,2,0:T(2,128)S(1)}, f32[8,16,2,128]{3,2,1,0:T(2,128)S(1)}, f32[16,8,16,2]{2,3,1,0:T(2...) while((s32[]{:T(128)}, f32[8,16,2]{1,2,0:T(2,128)S(1)}, ...), condition=%wide.region_5.6_spmd, body=%wide.region_4.5_spmd.sunk | while | flops 99845 | bytes 669847 | solution.py:20
  482.7 0.9 constant_dynamic-slice_fusion.2
  484.7 0.9 constant_dynamic-slice_fusion.2
  486.8 0.9 constant_dynamic-slice_fusion.2
  488.8 0.9 constant_dynamic-slice_fusion.2
  490.8 0.9 constant_dynamic-slice_fusion.2
  492.8 0.9 constant_dynamic-slice_fusion.2
  494.9 0.9 constant_dynamic-slice_fusion.2
  496.9 0.9 constant_dynamic-slice_fusion.2
  498.9 0.9 constant_dynamic-slice_fusion.2
  500.9 0.9 constant_dynamic-slice_fusion.2
  503.0 0.9 constant_dynamic-slice_fusion.2
  505.0 0.9 constant_dynamic-slice_fusion.2
  507.0 0.9 constant_dynamic-slice_fusion.2
  509.0 0.9 constant_dynamic-slice_fusion.2
  511.1 0.9 constant_dynamic-slice_fusion.2
  513.8 68.4 %all_gather.30 = bf16[256,128]{1,0:T(8,128)(2,1)S(1)} all-gather(bf16[8,128]{1,0:T(8,128)(2,1)S(1)} %get-tuple-element.267), channel_id=1, replica_groups=mesh['row'=32,'col'=16] {'row'}, dimensions={0}, use_global_device_ids=true | all-gather | bytes 67584 | tf_op jit(solution)/shard_map/all_gather | solution.py:168
  582.2 2.1 convolution_bitcast_fusion
  584.3 6.9 copy.170
  591.2 5.1 gather_fusion
  596.3 1.3 copy.171
  598.0 83.8 %all-reduce = bf16[256]{0:T(256)(128)(2,1)S(1)} all-reduce(bf16[256]{0:T(256)(128)(2,1)S(1)} %dynamic-update-slice), channel_id=1, replica_groups=mesh['row'=32,'col'=16] {'row'}, use_global_device_ids=true, to_apply=%add | all-reduce | flops 256 | bytes 1024
  681.9 33.7 %all-reduce.2 = (f32[256]{0:T(256)S(1)}, f32[256,8]{0,1:T(8,128)S(1)}) all-reduce(bf16[256]{0:T(256)(128)(2,1)S(1)} %all-reduce, f32[256,8]{0,1:T(8,128)S(1)} %fusion.62), channel_id=1, replica_groups=mesh['row'=32,'col'=16] {'col'}, use_global_device_ids=true, to_apply=%region_8.9 | all-reduce | flops 2304 | bytes 17920 | tf_op jit(solution)/shard_map/psum | solution.py:182
  715.9 36.3 %all-reduce.6.cloned.1.call-done = f32[256,2,2,176]{0,3,2,1:T(8,128)} async-done(((f32[256,2,2,176]{0,3,2,1:T(8,128)}), f32[256,2,2,176]{0,3,2,1:T(8,128)}) %all-reduce.6.cloned.1.call-update) | async-done | bytes 720912 | tf_op jit(solution)/shard_map/psum | solution.py:182
  752.2 1.6 convolution_bitcast_fusion.1
  753.8 1.6 copy.174
  755.4 2.9 gather_fusion.1
  758.3 1.0 multiply_reduce_fusion.2
  760.7 1.8 copy.198
  762.6 5.2 gather_fusion.3
  767.7 2.5 copy.185
  770.2 321.7 %all-reduce.8.cloned.1.call-done = f32[256,128]{1,0:T(8,128)} async-done(((f32[256,128]{1,0:T(8,128)}), f32[256,128]{1,0:T(8,128)}) %all-reduce.8.cloned.1.call-update) | async-done | bytes 131088
  1092.0 1.3 dynamic-slice_add_fusion
  (194 shorter events, 29.0 us)
Async XLA Ops:
  7.2 506.3 %copy-start = (bf16[4096,128]{1,0:T(8,128)(2,1)S(1)}, bf16[4096,128]{1,0:T(8,128)(2,1)}, u32[]{:S(2)}) copy-start(bf16[4096,128]{1,0:T(8,128)(2,1)} %param.23) | copy-start | bytes 3145732
  7.2 2.6 copy-start.8
  7.2 3.0 copy-start.16
  7.2 3.1 copy-start.18
  7.2 474.4 %all-gather.5.cloned.1.call-start = ((), (), s32[]{:S(2)}) async-start(), calls=%async_computation.2 | async-start | bytes 2228224 | tf_op jit(solution)/shard_map/all_gather | solution.py:15
  9.7 1.3 copy-start.7
  10.3 1.3 copy-start.10
  10.9 1.7 copy-start.5
  11.2 1.3 copy-start.1
  12.6 6.8 copy-start.3
  12.6 6.8 copy-start.4
  12.7 6.9 copy-start.17
  12.7 7.0 copy-start.14
  208.9 551.8 %all-to-all-start = ((bf16[32,44,3,128]{3,1,2,0:T(8,128)(2,1)}), bf16[32,44,3,128]{3,1,2,0:T(8,128)(2,1)}, u32[]{:S(2)}, u32[]{:S(2)}) async-start(bf16[32,44,3,128]{3,1,2,0:T(8,128)(2,1)} %copy.179), calls=%async_computation | async-start | bytes 2359296 | tf_op jit(solution)/shard_map/all_to_all | solution.py:120
  228.3 523.8 %all-reduce.6.cloned.1.call-start = ((), (), s32[]{:S(2)}) async-start(), calls=%async_computation.1 | async-start | bytes 1441792 | tf_op jit(solution)/shard_map/psum | solution.py:182
  393.9 9.7 copy-start.19
  393.9 44.1 %copy-start.6 = (f32[8,16,2]{0,2,1:T(2,128)S(1)}, f32[8,16,2]{0,2,1:T(2,128)}, u32[]{:S(2)}) copy-start(f32[8,16,2]{0,2,1:T(2,128)} %copy-done.5) | copy-start | bytes 3076
  393.9 44.4 %copy-start.11 = (pred[8,8]{1,0:T(8,128)(4,1)S(1)}, pred[8,8]{1,0:T(8,128)(4,1)}, u32[]{:S(2)}) copy-start(pred[8,8]{1,0:T(8,128)(4,1)} %copy-done.10) | copy-start | bytes 196
  393.9 75.4 %copy-start.9 = (s32[256,2]{0,1:T(2,128)S(1)}, s32[256,2]{0,1:T(2,128)}, u32[]{:S(2)}) copy-start(s32[256,2]{0,1:T(2,128)} %param.29) | copy-start | bytes 6148
  438.0 42.1 %copy-start.15 = (u32[512]{0:T(512)S(1)}, u32[512]{0:T(512)}, u32[]{:S(2)}) copy-start(u32[512]{0:T(512)} %constant.216) | copy-start | bytes 6148
  482.6 30.8 %copy-start.12 = (bf16[8,128]{1,0:T(8,128)(2,1)S(1)}, bf16[8,128]{1,0:T(8,128)(2,1)}, u32[]{:S(2)}) copy-start(bf16[8,128]{1,0:T(8,128)(2,1)} %param.17) | copy-start | bytes 6148
  513.0 69.2 %copy-start.2 = (bf16[8,176,3,128]{3,1,2,0:T(8,128)(2,1)S(1)}, bf16[8,176,3,128]{3,1,2,0:T(8,128)(2,1)}, u32[]{:S(2)}) copy-start(bf16[8,176,3,128]{3,1,2,0:T(8,128)(2,1)} %param.26) | copy-start | bytes 3244036
  596.3 85.5 %copy-start.13 = (bf16[128,8]{0,1:T(8,128)(2,1)S(1)}, bf16[128,8]{0,1:T(8,128)(2,1)}, u32[]{:S(2)}) copy-start(bf16[128,8]{0,1:T(8,128)(2,1)} %param.25) | copy-start | bytes 6148
  597.7 494.3 %all-reduce.8.cloned.1.call-start = ((), (), s32[]{:S(2)}) async-start(), calls=%async_computation.3 | async-start | bytes 262144
Sparse Core Ops, SparseCore 0:
  12.7 75.4 all-gather.4
  597.8 154.3 all-reduce.5
  759.4 332.4 all-reduce.7
where the time goes:
time: 1100 us
  local copies, waits for them, and re-layouts  415 us (38%)
  waiting for transfers between devices  358 us (33%)
  blocking collectives  251 us (23%)
  other arithmetic  33.2 us (3%)
  starting transfers between devices  19.6 us (2%)
  between operations  15.8 us (1%)
    unnamed x52, local copies, waits for them, and re-layouts  336 us
    unnamed x4, waiting for transfers between devices  322 us
    unnamed x1, blocking collectives  83.8 us
    all_gather x1, blocking collectives, local(): lax.all_gather(scaled, 'row', axis=0, tiled=True)  68.4 us
    all_gather x2, blocking collectives, joined(): gathered = jax.tree.map(lambda a: lax.all_gather(a, axis), part)  64.9 us
    psum x1, waiting for transfers between devices, local(): lax.psum((picked, router_part, every_square), 'col')  36.3 us
    psum x1, blocking collectives, local(): lax.psum((picked, router_part, every_square), 'col')  33.7 us
  transfers between devices with their start and end apart: 4, of which 2 were waited for; matrix products, arithmetic and copies ran while one was open for 41% of the time, Pallas kernels for 0%

commit v1 on v0

--- a/solution.py
+++ b/solution.py
@@ -165,7 +165,9 @@
     scaled = (h_float * moe_gain.astype(jnp.float32)[None, :]).astype(jnp.bfloat16)
     squares = jnp.sum(h_float * h_float, axis=1)
     every_token, every_square = (
-        lax.all_gather(scaled, "row", axis=0, tiled=True),
+        jnp.concatenate(
+            lax.all_to_all(jnp.stack([scaled] * lax.axis_size("row")), "row", 0, 0), axis=0
+        ),
         lax.all_gather(squares.astype(jnp.bfloat16), "row", axis=0, tiled=True).astype(
             squares.dtype
         ),

time: 1100 us -> 1150 us (1.045)
  waiting for transfers between devices: 358 us -> 456 us
  blocking collectives: 251 us -> 188 us
  starting transfers between devices: 19.6 us -> 36.2 us
    psum x1, waiting for transfers between devices: 36.3 us -> 128 us  [local(): lax.psum((picked, router_part, every_square), 'col')]
    all_gather x1 -> x0, blocking collectives: 68.4 us -> none  [local(): lax.all_gather(scaled, 'row', axis=0, tiled=True)]
    all_to_all x0 -> x1, starting transfers between devices: none -> 28.3 us  [local(): lax.all_to_all(jnp.stack([scaled] * lax.axis_size('row')), 'row', 0, 0)]
    all_to_all x1, starting transfers between devices: 19.4 us -> 7.78 us  [migrate(): lax.all_to_all(outgoing, 'row', split_axis=0, concat_axis=0, tiled=True)]
    unnamed x52 -> x46, local copies, waits for them, and re-layouts: 336 us -> 336 us
  transfers between devices with their start and end apart: 4 -> 5, of which waited for: 2 -> 3; matrix products, arithmetic and copies ran while one was open for 41% -> 36% of each run, Pallas kernels for 0% -> 0%
where the time goes in v1:
time: 1150 us
  waiting for transfers between devices  456 us (40%)
  local copies, waits for them, and re-layouts  415 us (36%)
  blocking collectives  188 us (16%)
  starting transfers between devices  36.2 us (3%)
  other arithmetic  33.6 us (3%)
  between operations  15.8 us (1%)
    unnamed x46, local copies, waits for them, and re-layouts  336 us
    unnamed x4, waiting for transfers between devices  322 us
    psum x1, waiting for transfers between devices, local(): lax.psum((picked, router_part, every_square), 'col')  128 us
    unnamed x1, blocking collectives  84.1 us
    all_gather x2, blocking collectives, joined(): gathered = jax.tree.map(lambda a: lax.all_gather(a, axis), part)  70.1 us
    psum x1, blocking collectives, local(): lax.psum((picked, router_part, every_square), 'col')  34.1 us
    all_to_all x1, starting transfers between devices, local(): lax.all_to_all(jnp.stack([scaled] * lax.axis_size('row')), 'row', 0, 0)  28.3 us
  transfers between devices with their start and end apart: 5, of which 3 were waited for; matrix products, arithmetic and copies ran while one was open for 36% of the time, Pallas kernels for 0%

profile of v1, /device:TPU:1, one launch (start us, length us, event | category | flops | bytes accessed | tf_op | source)
XLA Modules:
  0.0 1153.4 jit_solution(12342489374919547473)
XLA Ops:
  7.3 1.2 fusion.40
  8.6 1.1 slice_bitcast_fusion.2
  13.1 38.4 %all-gather = f32[128,16,2]{1,2,0:T(2,128)S(1)} all-gather(f32[8,16,2]{1,2,0:T(2,128)S(1)} %copy.156), channel_id=2, replica_groups=mesh['row'=32,'col'=16] {'col'}, dimensions={0}, use_global_device_ids=true | all-gather | bytes 17408 | tf_op jit(solution)/shard_map/all_gather | solution.py:15
  52.3 31.7 %all-gather.1 = f32[128,16,2]{1,2,0:T(2,128)S(1)} all-gather(f32[8,16,2]{1,2,0:T(2,128)S(1)} %copy.161), channel_id=3, replica_groups=mesh['row'=32,'col'=16] {'col'}, dimensions={0}, use_global_device_ids=true | all-gather | bytes 17408 | tf_op jit(solution)/shard_map/all_gather | solution.py:15
  84.2 6.7 copy.177
  92.8 165.0 %scatter_custom_fusion = s32[45056]{0:T(1024)S(1)} fusion(s32[45056]{0:T(1024)} %reshape.250, s32[45056]{0:T(1024)} %reshape.252, s32[]{:T(128)} %constant.115.clone.1), kind=kCustom, calls=%fused_computation.72 | custom fusion | bytes 180736
  258.7 8.6 gather_fusion.4
  267.6 5.0 sort.17
  273.6 30.3 %while.19 = (s32[]{:T(128)}, f32[8,16,2]{1,2,0:T(2,128)S(1)}, f32[8,16,2]{1,2,0:T(2,128)S(1)}, f32[8,16,2,128]{3,2,1,0:T(2,128)S(1)}, f32[16,8,16,2]{2,3,1,0:T(2...) while((s32[]{:T(128)}, f32[8,16,2]{1,2,0:T(2,128)S(1)}, ...), condition=%wide.region_5.6_spmd, body=%wide.region_4.5_spmd.sunk | while | flops 99845 | bytes 669847 | solution.py:20
  273.7 0.9 constant_dynamic-slice_fusion.2
  275.7 0.9 constant_dynamic-slice_fusion.2
  277.7 0.9 constant_dynamic-slice_fusion.2
  279.8 0.9 constant_dynamic-slice_fusion.2
  281.8 0.9 constant_dynamic-slice_fusion.2
  283.8 0.9 constant_dynamic-slice_fusion.2
  285.8 0.9 constant_dynamic-slice_fusion.2
  287.8 0.9 constant_dynamic-slice_fusion.2
  289.9 0.9 constant_dynamic-slice_fusion.2
  291.9 0.9 constant_dynamic-slice_fusion.2
  293.9 0.9 constant_dynamic-slice_fusion.2
  295.9 0.9 constant_dynamic-slice_fusion.2
  297.9 0.9 constant_dynamic-slice_fusion.2
  299.9 0.9 constant_dynamic-slice_fusion.2
  302.0 0.9 constant_dynamic-slice_fusion.2
  305.4 28.3 %all-to-all-start = ((bf16[32,8,128]{2,1,0:T(8,128)(2,1)}), bf16[32,8,128]{2,1,0:T(8,128)(2,1)S(1)}, u32[]{:S(2)}, u32[]{:S(2)}) async-start(bf16[32,8,128]{2,1,0:T(8,128)(2,1)} %stack.2), calls=%async_computation | async-start | bytes 131072 | tf_op jit(solution)/shard_map/all_to_all | solution.py:169
  333.6 5.2 gather_fusion.2
  338.8 2.6 copy.179
  341.4 6.9 all-to-all-done
  348.2 7.8 all-to-all-start.1
  356.1 165.3 %scatter_custom_fusion.1 = s32[45056]{0:T(1024)S(1)} fusion(s32[45056]{0:T(1024)S(1)} %reshape.256, s32[45056]{0:T(1024)} %reshape.252, s32[]{:T(128)} %constant.115.clone.1), kind=kCustom, calls=%fused_computation.70 | custom fusion | bytes 180736
  521.6 8.6 gather_fusion.5
  532.5 9.1 reduce-window.6
  543.8 84.1 %all-reduce = bf16[256]{0:T(256)(128)(2,1)S(1)} all-reduce(bf16[256]{0:T(256)(128)(2,1)S(1)} %dynamic-update-slice), channel_id=1, replica_groups=mesh['row'=32,'col'=16] {'row'}, use_global_device_ids=true, to_apply=%add | all-reduce | flops 256 | bytes 1024
  627.9 2.1 convolution_bitcast_fusion
  630.1 6.9 copy.170
  636.9 5.1 gather_fusion
  642.1 1.3 copy.171
  643.6 34.1 %all-reduce.2 = (f32[256]{0:T(256)S(1)}, f32[256,8]{0,1:T(8,128)S(1)}) all-reduce(bf16[256]{0:T(256)(128)(2,1)S(1)} %all-reduce, f32[256,8]{0,1:T(8,128)S(1)} %fusion.36), channel_id=1, replica_groups=mesh['row'=32,'col'=16] {'col'}, use_global_device_ids=true, to_apply=%region_8.9 | all-reduce | flops 2304 | bytes 17920 | tf_op jit(solution)/shard_map/psum | solution.py:184
  677.9 127.8 %all-reduce.6.cloned.1.call-done = f32[256,2,2,176]{0,3,2,1:T(8,128)} async-done(((f32[256,2,2,176]{0,3,2,1:T(8,128)}), f32[256,2,2,176]{0,3,2,1:T(8,128)}) %all-reduce.6.cloned.1.call-update) | async-done | bytes 720912 | tf_op jit(solution)/shard_map/psum | solution.py:184
  805.7 1.6 convolution_bitcast_fusion.1
  807.3 1.6 copy.174
  808.9 2.9 gather_fusion.1
  811.8 1.0 multiply_reduce_fusion.2
  814.2 1.8 copy.198
  816.1 5.2 gather_fusion.3
  821.3 2.5 copy.185
  823.8 321.8 %all-reduce.8.cloned.1.call-done = f32[256,128]{1,0:T(8,128)} async-done(((f32[256,128]{1,0:T(8,128)}), f32[256,128]{1,0:T(8,128)}) %all-reduce.8.cloned.1.call-update) | async-done | bytes 131088
  1145.6 1.3 dynamic-slice_add_fusion
  (190 shorter events, 31.0 us)
Async XLA Ops:
  7.2 297.2 %copy-start = (bf16[4096,128]{1,0:T(8,128)(2,1)S(1)}, bf16[4096,128]{1,0:T(8,128)(2,1)}, u32[]{:S(2)}) copy-start(bf16[4096,128]{1,0:T(8,128)(2,1)} %param.23) | copy-start | bytes 3145732
  7.2 2.6 copy-start.6
  7.2 3.0 copy-start.13
  7.2 3.1 copy-start.15
  7.2 265.4 %all-gather.5.cloned.1.call-start = ((), (), s32[]{:S(2)}) async-start(), calls=%async_computation.3 | async-start | bytes 2228224 | tf_op jit(solution)/shard_map/all_gather | solution.py:15
  9.7 1.3 copy-start.5
  11.2 1.3 copy-start.16
  11.2 40.2 %copy-start.3 = (s32[8,5632]{1,0:T(8,128)S(1)}, s32[8,5632]{1,0:T(8,128)}, u32[]{:S(2)}) copy-start(s32[8,5632]{1,0:T(8,128)} %param.27) | copy-start | bytes 540676
  11.6 72.5 %copy-start.1 = (bf16[8,176,3,128]{3,1,2,0:T(8,128)(2,1)S(1)}, bf16[8,176,3,128]{3,1,2,0:T(8,128)(2,1)}, u32[]{:S(2)}) copy-start(bf16[8,176,3,128]{3,1,2,0:T(8,128)(2,1)} %param.26) | copy-start | bytes 3244036
  84.2 6.8 copy-start.4
  84.2 6.8 copy-start.11
  84.2 6.9 copy-start.14
  273.6 30.7 %copy-start.8 = (bf16[8,128]{1,0:T(8,128)(2,1)S(1)}, bf16[8,128]{1,0:T(8,128)(2,1)}, u32[]{:S(2)}) copy-start(bf16[8,128]{1,0:T(8,128)(2,1)} %param.17) | copy-start | bytes 6148
  273.6 30.7 %copy-start.10 = (f32[128]{0:T(128)S(1)}, f32[128]{0:T(128)}, u32[]{:S(2)}) copy-start(f32[128]{0:T(128)} %convert_element_type.67) | copy-start | bytes 1540
  305.4 42.9 %all-to-all-start = ((bf16[32,8,128]{2,1,0:T(8,128)(2,1)}), bf16[32,8,128]{2,1,0:T(8,128)(2,1)S(1)}, u32[]{:S(2)}, u32[]{:S(2)}) async-start(bf16[32,8,128]{2,1,0:T(8,128)(2,1)} %stack.2), calls=%async_computation | async-start | bytes 131072 | tf_op jit(solution)/shard_map/all_to_all | solution.py:169
  348.2 466.0 %all-to-all-start.1 = ((bf16[32,44,3,128]{3,1,2,0:T(8,128)(2,1)}), bf16[32,44,3,128]{3,1,2,0:T(8,128)(2,1)}, u32[]{:S(2)}, u32[]{:S(2)}) async-start(bf16[32,44,3,128]{3,1,2,0:T(8,128)(2,1)} %copy.179), calls=%async_computation.1 | async-start | bytes 2359296 | tf_op jit(solution)/shard_map/all_to_all | solution.py:120
  356.0 449.7 %all-reduce.6.cloned.1.call-start = ((), (), s32[]{:S(2)}) async-start(), calls=%async_computation.2 | async-start | bytes 1441792 | tf_op jit(solution)/shard_map/psum | solution.py:184
  521.5 9.7 copy-start.7
  530.1 11.9 %copy-start.12 = (u32[512]{0:T(512)S(1)}, u32[512]{0:T(512)}, u32[]{:S(2)}) copy-start(u32[512]{0:T(512)} %constant.216) | copy-start | bytes 6148
  531.4 96.6 %copy-start.2 = (bf16[8,176,3,128]{3,1,2,0:T(8,128)(2,1)S(1)}, bf16[8,176,3,128]{3,1,2,0:T(8,128)(2,1)}, u32[]{:S(2)}) copy-start(bf16[8,176,3,128]{3,1,2,0:T(8,128)(2,1)} %param.26) | copy-start | bytes 3244036
  642.1 1.4 copy-start.9
  643.4 502.2 %all-reduce.8.cloned.1.call-start = ((), (), s32[]{:S(2)}) async-start(), calls=%async_computation.4 | async-start | bytes 262144
Sparse Core Ops, SparseCore 0:
  12.7 77.0 all-gather.4
  643.5 162.1 all-reduce.5
  813.0 332.5 all-reduce.7
